TPU v7x, 32 devices: a whole 2x2x4 slice. The times are simulated.
32 devices in a mesh: pages: 8 (over z, core), blocks: 4 (over y, x).
Axes of the slice: x: 2, y: 2, z: 4, core: 2. Of those that a mesh axis runs over, the one named last changes fastest.
Arguments:
- queries: bfloat16 [64, 24, 128], P(('pages', 'blocks')), may hold values from -0.5 to 0.5
- centroids: bfloat16 [256, 128], replicated, may hold values from -6 to 6
- basis: bfloat16 [256, 32, 128], replicated, may hold values from -1 to 1
- patch_ids: int32 [8, 32, 256], P('pages', None, 'blocks'), may hold values from 0 to 255
- coeffs: bfloat16 [8, 32, 8192], P('pages', None, 'blocks'), may hold values from -6 to 6
- page_counts: int32 [8, 32], P('pages'), may hold values from 128 to 256
- cand_ids: int32 [8, 64, 16], P('pages'), may hold values from 0 to 31
- cand_counts: int32 [8, 64], P('pages'), may hold values from 0 to 16, as said below
Outputs:
- scores: float32 [64, 8, 16], P(('pages', 'blocks'))
Inputs may be any that keep to these rules, and one draw needn't show every extreme that they name: `cand_ids`: slots at or past a query's count in a group are padding and name arbitrary pages; ids may repeat. `cand_counts`: each query's counts over the 8 groups add up to 64.
All inputs are finite; a program needn't handle non-finite values.
Results may differ from a plain program's by a relative error of at most 0.00065.
Values may be sent and summed in bfloat16 or wider, within the bound.
A program may use at most 64 MiB of HBM per device.

v0:
```python
import functools

import jax
import jax.numpy as jnp
from jax import lax
from jax.experimental import pallas as pl
from jax.experimental.pallas import tpu as pltpu
from jax.sharding import PartitionSpec as P

MESH = pl.DeviceIdType.MESH
SPLIT = 4
STEP = 8
AHEAD, NEAR, FAR = 1, 3, 4
LOWEST = -3.0e38


def remote(src, dst, send, recv, where):
    return pltpu.make_async_remote_copy(
        src_ref=src, dst_ref=dst, send_sem=send, recv_sem=recv, device_id=where, device_id_type=MESH
    )


def flip(index, bits):
    for bit in range(bits.bit_length()):
        if bits >> bit & 1:
            index = index + 2**bit - 2 ** (bit + 1) * lax.rem(lax.div(index, 2**bit), 2)
    return index


def far_first(count):
    return sorted(range(1, count), key=lambda s: -s.bit_count())


def kernel(
    n_pages, n_blocks, qtok,
    q_hbm, cent_hbm, basis_hbm, ids_hbm, coef_hbm, count_hbm, cand_hbm, live_hbm, out_ref,
    cent, basis, ids, coef, count, cand, live,
    qbuf, idb, dlow, emb, first, bound, outgo, income, gather, scoreT, piece, landed,
    in_sem, z_send, z_recv, b_send, b_recv, c_send, c_recv, d_send, d_recv, e_send, e_recv,
):
    k = lax.axis_index("pages")
    r = lax.axis_index("blocks")
    core = lax.rem(k, 2)
    z = lax.div(k, 2)
    nz = n_pages // 2
    pages, patches = ids.shape
    cents, width = cent.shape
    rank = basis.shape[0] // cents
    rows_q = q_hbm.shape[0]
    cols = n_pages * rows_q

    barrier = pltpu.get_barrier_semaphore()
    for s in range(1, n_pages):
        pl.semaphore_signal(
            barrier, inc=1, device_id=(lax.rem(k + s, n_pages), r), device_id_type=MESH
        )
    for s in range(1, n_blocks):
        pl.semaphore_signal(
            barrier, inc=1, device_id=(k, lax.rem(r + s, n_blocks)), device_id_type=MESH
        )

    own = qbuf.at[r, core, pl.ds(pl.multiple_of(z * rows_q, rows_q), rows_q), :]
    loads = [
        pltpu.make_async_copy(src, dst, in_sem.at[i])
        for i, (src, dst) in enumerate(
            [
                (ids_hbm, ids), (count_hbm, count), (q_hbm, own), (coef_hbm, coef),
                (cent_hbm, cent), (basis_hbm, basis), (cand_hbm, cand), (live_hbm, live),
            ]
        )
    ]
    for copy in loads:
        copy.start()

    loads[0].wait()
    loads[1].wait()
    low_total = cents // SPLIT
    lane_cent = lax.div(lax.broadcasted_iota(jnp.int32, (1, STEP * width), 1), rank)
    lane_cent = lax.rem(lane_cent, width // rank).astype(jnp.float32)
    id_f = ids[...].astype(jnp.float32)
    id_low = lax.bitwise_and(ids[...], low_total - 1).astype(jnp.float32)
    id_both = jnp.concatenate([id_f, id_low], axis=0).astype(jnp.bfloat16)
    to_col = lax.div(lax.broadcasted_iota(jnp.int32, (1, STEP * width), 1), width)
    from_row = lax.broadcasted_iota(jnp.int32, (STEP, STEP * width), 0)
    pick = (from_row == to_col).astype(jnp.float32).astype(jnp.bfloat16)
    for m in range(patches // STEP):
        wide = jnp.dot(
            id_both[:, m * STEP : (m + 1) * STEP], pick, preferred_element_type=jnp.float32
        )
        wide_id = wide[:pages].astype(jnp.bfloat16)
        wide_low = (wide[pages:] - lane_cent).astype(jnp.bfloat16)
        for p in range(STEP):
            idb[m * STEP + p] = wide_id[:, p * width : (p + 1) * width]
            dlow[m * STEP + p] = wide_low[:, p * width : (p + 1) * width]
    spread = jnp.broadcast_to(count[...].astype(jnp.float32), (pages, pages))
    diag = lax.broadcasted_iota(jnp.int32, (pages, pages), 0) == lax.broadcasted_iota(
        jnp.int32, (pages, pages), 1
    )
    column = jnp.sum(jnp.where(diag, spread, 0.0), axis=1, keepdims=True)
    bound[...] = jnp.broadcast_to(column, (pages, width)) - (r * patches).astype(jnp.float32)

    for copy in loads[3:]:
        copy.wait()

    n_query = cand.shape[1]
    per_dev = rows_q // qtok
    spot = lax.broadcasted_iota(jnp.int32, (1, cols), 1)
    seen = lax.broadcasted_iota(jnp.int32, (n_query, cols), 0)
    shard = lax.div(spot, rows_q)
    owner = lax.rem(shard, nz) * 2 + lax.div(shard, nz)
    index = (owner * n_blocks + r) * per_dev + lax.div(lax.rem(spot, rows_q), qtok)
    gather[...] = (index == seen).astype(jnp.float32).astype(jnp.bfloat16)

    per = width // rank
    tile_row = lax.broadcasted_iota(jnp.int32, (width, per * width), 0)
    tile_col = lax.broadcasted_iota(jnp.int32, (1, per * width), 1)
    tile = (
        (tile_row == lax.div(tile_col, width) * rank + lax.rem(tile_col, rank))
        .astype(jnp.float32)
        .astype(jnp.bfloat16)
    )
    depth = low_total * rank
    rows = STEP * pages

    def decode(m):
        base = m * STEP
        parts = []
        for h in range(STEP // per):
            chunk = coef[:, pl.ds(pl.multiple_of((m * (STEP // per) + h) * width, width), width)]
            spreadc = jnp.dot(chunk, tile, preferred_element_type=jnp.float32)
            for s in range(per):
                parts.append(spreadc[:, s * width : (s + 1) * width].astype(jnp.bfloat16))
        weights = jnp.concatenate(parts, axis=0)
        low = dlow[pl.ds(base, STEP)].reshape(rows, width)
        mine = idb[pl.ds(base, STEP)].reshape(rows, width)
        zero = jnp.zeros((rows, width), jnp.bfloat16)
        lhs = jnp.concatenate(
            [
                jnp.where(low == jnp.bfloat16(per * t), weights, zero)
                for t in range(depth // width)
            ],
            axis=1,
        )
        rhs = jnp.concatenate(
            [basis[h * depth : (h + 1) * depth, :] for h in range(SPLIT)], axis=1
        )
        res = jnp.dot(lhs, rhs, preferred_element_type=jnp.float32)
        lane_id = lax.broadcasted_iota(jnp.int32, (rows, width), 1).astype(jnp.float32).astype(jnp.bfloat16)
        one = jnp.ones((rows, width), jnp.bfloat16)
        hot = jnp.concatenate(
            [
                jnp.where(mine == lane_id + jnp.bfloat16(t * width), one, zero)
                for t in range(cents // width)
            ],
            axis=1,
        )
        center = jnp.dot(hot, cent[...], preferred_element_type=jnp.float32)
        mine_f = mine.astype(jnp.float32)
        total = res[:, :width]
        for h in range(1, SPLIT):
            total = jnp.where(
                mine_f >= float(h * low_total), res[:, h * width : (h + 1) * width], total
            )
        total = (total + center).reshape(STEP, pages, width)

        @pl.when(m == 0)
        def _():
            first[...] = total[0]

        position = base + lax.broadcasted_iota(jnp.int32, (STEP, pages, width), 0)
        valid = position.astype(jnp.float32) < bound[...][None]
        total = jnp.where(valid, total, first[...][None])
        emb[pl.ds(pl.multiple_of(m * rows, rows), rows), :] = total.astype(jnp.bfloat16).reshape(rows, width)

    turns = patches // STEP

    def decode_steps(start, stop):
        start, stop = min(start, turns), min(stop, turns)
        if stop > start:
            lax.fori_loop(start, stop, lambda m, carry: (decode(m), carry)[1], 0)

    def shard_at(block, where):
        return qbuf.at[block, core, pl.ds(pl.multiple_of(where * rows_q, rows_q), rows_q), :]

    decode_steps(0, AHEAD)
    loads[2].wait()
    pl.semaphore_wait(barrier, n_pages - 1 + n_blocks - 1)
    z_copies = {
        s: remote(own, own, z_send.at[s], z_recv.at[s], (flip(z, s) * 2 + core, r))
        for s in far_first(nz)
    }
    for copy in z_copies.values():
        copy.start()
    b_copies = {}

    def forward(t):
        if t:
            z_copies[t].wait_recv()
        part = shard_at(r, flip(z, t))
        for s in far_first(n_blocks):
            b_copies[s, t] = remote(
                part, part, b_send.at[s, t], b_recv.at[s, t], (k, flip(r, s))
            )
            b_copies[s, t].start()

    forward(0)
    decode_steps(AHEAD, NEAR)
    for t in range(1, nz // 2 + 1):
        forward(t)
    decode_steps(NEAR, FAR)
    for t in range(nz // 2 + 1, nz):
        forward(t)
    partner = (k + 1 - 2 * core, r)

    def share(s):
        for t in range(nz):
            if s:
                b_copies[s, t].wait_recv()
        half = qbuf.at[flip(r, s), core]
        copy = remote(half, half, c_send.at[s], c_recv.at[s], partner)
        copy.start()
        return copy

    c_copies = {0: share(0)}
    decode_steps(FAR, turns)

    def best_of(source):
        query = qbuf[source].reshape(cols, width)

        best = jnp.full((pages, cols), LOWEST, jnp.float32)
        for m in range(turns):
            sim = lax.dot_general(
                emb[m * rows : (m + 1) * rows, :], query, (((1,), (1,)), ((), ())),
                preferred_element_type=jnp.float32,
            )
            best = jnp.maximum(best, jnp.max(sim.reshape(STEP, pages, cols), axis=0))
        return jnp.where(bound[:, :1] > 0.0, best, LOWEST).astype(jnp.bfloat16)

    c_copies[0].wait_recv()
    income[0] = best_of(r)
    for s in far_first(n_blocks):
        c_copies[s] = share(s)
    d_copies = []
    for s in far_first(n_blocks):
        c_copies[s].wait_recv()
        source = flip(r, s)
        outgo[s] = best_of(source)
        copy = remote(outgo.at[s], income.at[s], d_send.at[s], d_recv.at[s], (k, source))
        copy.start()
        d_copies.append(copy)

    slots = cand.shape[0]
    used = lax.broadcasted_iota(jnp.int32, (slots, n_query), 0) < live[...]
    chosen = cand[...]

    highest = income[0].astype(jnp.float32)
    for copy in d_copies:
        copy.wait_recv()
    for s in range(1, n_blocks):
        highest = jnp.maximum(highest, income[s].astype(jnp.float32))
    sums = lax.dot_general(
        highest.astype(jnp.bfloat16), gather[...], (((1,), (1,)), ((), ())),
        preferred_element_type=jnp.float32,
    )
    picked = jnp.zeros((slots, n_query), jnp.float32)
    for n in range(pages):
        picked = jnp.where(chosen == n, sums[n : n + 1, :], picked)
    picked = jnp.where(used, picked, 0.0)
    wide_q = scoreT.shape[0]
    padded = picked
    if wide_q > n_query:
        padded = jnp.concatenate([padded, jnp.zeros((slots, wide_q - n_query), jnp.float32)], axis=1)
    full = jnp.concatenate([padded, jnp.zeros((width - slots, wide_q), jnp.float32)], axis=0)
    scoreT[...] = full.T

    e_copies = []
    for s in range(n_pages - 1, -1, -1):
        to = flip(k, s)
        values = scoreT[pl.ds((to * n_blocks + r) * per_dev, per_dev), :]
        if s == 0:
            landed[k] = values
        else:
            piece[s] = values
            copy = remote(piece.at[s], landed.at[k], e_send.at[s], e_recv.at[s], (to, r))
            copy.start()
            e_copies.append(copy)
    for copy in e_copies:
        copy.wait_recv()
    for g in range(n_pages):
        arrived = landed[g]
        for i in range(per_dev):
            out_ref[i, g : g + 1, :] = arrived[i : i + 1, :slots]
    started = [*z_copies.values(), *b_copies.values(), *c_copies.values(), *d_copies, *e_copies]
    for copy in started:
        copy.wait_send()


def on_device(queries, centroids, basis, patch_ids, coeffs, page_counts, cand_ids, cand_counts):
    n_pages = lax.axis_size("pages")
    n_blocks = lax.axis_size("blocks")
    owned, qtok, width = queries.shape
    cents, rank, _ = basis.shape
    _, pages, patches = patch_ids.shape
    _, n_query, slots = cand_ids.shape
    rows_q = owned * qtok
    cols = n_pages * rows_q
    args = (
        queries.reshape(rows_q, width),
        centroids,
        basis.reshape(cents * rank, width),
        patch_ids[0],
        coeffs[0],
        page_counts,
        jnp.swapaxes(cand_ids[0], 0, 1),
        cand_counts,
    )
    dma = pltpu.SemaphoreType.DMA
    bf16, f32 = jnp.bfloat16, jnp.float32
    vmem = pltpu.VMEM
    totals = pl.pallas_call(
        functools.partial(kernel, n_pages, n_blocks, qtok),
        out_shape=jax.ShapeDtypeStruct((owned, n_pages, slots), f32),
        in_specs=[pl.BlockSpec(memory_space=pl.ANY)] * len(args),
        out_specs=pl.BlockSpec(memory_space=pltpu.VMEM),
        scratch_shapes=[vmem(a.shape, a.dtype) for a in args[1:]]
        + [
            vmem((n_blocks, 2, cols // 2, width), bf16),
            vmem((patches, pages, width), bf16),
            vmem((patches, pages, width), bf16),
            vmem((patches * pages, width), bf16),
            vmem((pages, width), f32),
            vmem((pages, width), f32),
            vmem((n_blocks, pages, cols), bf16),
            vmem((n_blocks, pages, cols), bf16),
            vmem((n_query, cols), bf16),
            vmem((-(-n_query // 128) * 128, width), f32),
            vmem((n_pages, owned, width), f32),
            vmem((n_pages, owned, width), f32),
            dma((len(args),)),
            dma((n_pages,)), dma((n_pages,)),
            dma((n_blocks, n_pages // 2)), dma((n_blocks, n_pages // 2)),
            dma((n_blocks,)), dma((n_blocks,)),
            dma((n_blocks,)), dma((n_blocks,)),
            dma((n_pages,)), dma((n_pages,)),
        ],
        compiler_params=pltpu.CompilerParams(collective_id=0, has_side_effects=True),
    )(*args)
    return totals / qtok


def solution(mesh):
    placed = (
        P(("pages", "blocks"), None, None),
        P(),
        P(),
        P("pages", None, "blocks"),
        P("pages", None, "blocks"),
        P("pages", None),
        P("pages", None, None),
        P("pages", None),
    )
    return jax.shard_map(
        on_device,
        mesh=mesh,
        in_specs=placed,
        out_specs=P(("pages", "blocks"), None, None),
        check_vma=False,
    )
```

profile of v0, /device:TPU:0, one launch (start us, length us, event | category | flops | bytes accessed | tf_op | source)
XLA Modules:
  0.0 25.1 jit_solution(15816497644584306678)
XLA Ops:
  0.0 23.8 %shard_map.82 = f32[2,8,16]{2,1,0:T(8,128)} custom-call(bf16[48,128]{1,0:T(8,128)(2,1)} %bitcast.10, bf16[256,128]{1,0:T(8,128)(2,1)} %cent_hbm.1, bf16[8192,128]{1,0:T(8,128)(2,1)} %bitcast.7, s32[32,64]{1,0:T(8,128)} %bitcast.9, bf16[32,2048]{1,0:T(8,128)(2,1)} %bitcast.8, s32[1,32]{1,0:T(1,128)} %count_hbm.1, s32[16,64]{1,0:T(8,128)} %bitcast.11, ...), custom_call_target="tpu_custom_call" | custom-call | tf_op jit(solution)/shard_map/pallas_call | solution.py:320
  23.8 1.3 %broadcast_multiply_fusion = f32[2,8,16]{2,1,0:T(8,128)} fusion(f32[2,8,16]{2,1,0:T(8,128)} %shard_map.82), kind=kLoop, calls=%fused_computation | loop fusion | flops 256 | bytes 2048 | tf_op jit(solution)/shard_map/div | solution.py:348
where the time goes:
time: 25.3 us; the launch traced here: 25.1 us
  Pallas kernels  23.8 us (94%)
  other arithmetic  1.3 us (5%)
    pallas_call x1, Pallas kernels, on_device(): pl.pallas_call(functools.partial(kernel, n_pages, n_blocks, qtok), out_sh...  23.8 us
    div x1, other arithmetic, on_device(): return totals / qtok  1.3 us

commit v1 on v0

--- a/solution.py
+++ b/solution.py
@@ -319,7 +319,7 @@
     vmem = pltpu.VMEM
     totals = pl.pallas_call(
         functools.partial(kernel, n_pages, n_blocks, qtok),
-        out_shape=jax.ShapeDtypeStruct((owned, n_pages, slots), f32),
+        out_shape=vmem((owned, n_pages, slots), f32),
         in_specs=[pl.BlockSpec(memory_space=pl.ANY)] * len(args),
         out_specs=pl.BlockSpec(memory_space=pltpu.VMEM),
         scratch_shapes=[vmem(a.shape, a.dtype) for a in args[1:]]

time: 25.3 us -> 24 us (0.949)
  other arithmetic: 1.3 us -> 0.6 us
  Pallas kernels: 23.8 us -> 23.1 us
    div x1, other arithmetic: 1.3 us -> 0.6 us  [on_device(): return totals / qtok]
    pallas_call x1, Pallas kernels: 23.8 us -> 23.1 us  [on_device(): pl.pallas_call(functools.partial(kernel, n_pages, n_blocks, qtok), out_sh...]
where the time goes in v1:
time: 24 us; the launch traced here: 23.8 us
  Pallas kernels  23.1 us (96%)
  other arithmetic  0.6 us (2%)
    pallas_call x1, Pallas kernels, on_device(): pl.pallas_call(functools.partial(kernel, n_pages, n_blocks, qtok), out_sh...  23.1 us
    div x1, other arithmetic, on_device(): return totals / qtok  0.6 us

profile of v1, /device:TPU:0, one launch (start us, length us, event | category | flops | bytes accessed | tf_op | source)
XLA Modules:
  0.0 23.8 jit_solution(4718739833645702367)
XLA Ops:
  0.0 23.1 %shard_map.82 = f32[2,8,16]{2,1,0:T(8,128)S(1)} custom-call(bf16[48,128]{1,0:T(8,128)(2,1)} %bitcast.10, bf16[256,128]{1,0:T(8,128)(2,1)} %cent_hbm.1, bf16[8192,128]{1,0:T(8,128)(2,1)} %bitcast.7, s32[32,64]{1,0:T(8,128)} %bitcast.9, bf16[32,2048]{1,0:T(8,128)(2,1)} %bitcast.8, s32[1,32]{1,0:T(1,128)} %count_hbm.1, s32[16,64]{1,0:T(8,128)} %bitcast.11, ...), custom_call_target="tpu_custom_call" | custom-call | tf_op jit(solution)/shard_map/pallas_call | solution.py:320
  23.2 0.6 %broadcast_multiply_fusion = f32[2,8,16]{2,1,0:T(8,128)} fusion(f32[2,8,16]{2,1,0:T(8,128)S(1)} %shard_map.82), kind=kLoop, calls=%fused_computation | loop fusion | flops 256 | bytes 2048 | tf_op jit(solution)/shard_map/div | solution.py:348

commit v2 on v1

v2 whole, which is shorter than its diff:
```python
import functools

import jax
import jax.numpy as jnp
from jax import lax
from jax.experimental import pallas as pl
from jax.experimental.pallas import tpu as pltpu
from jax.sharding import PartitionSpec as P

MESH = pl.DeviceIdType.MESH
DEPTH = 256
GROUP = 384
STEP = 8
LOWEST = -3.0e38


def remote(src, dst, send, recv, where):
    return pltpu.make_async_remote_copy(
        src_ref=src, dst_ref=dst, send_sem=send, recv_sem=recv, device_id=where, device_id_type=MESH
    )


def arrived(ref, sem):
    pltpu.make_async_copy(ref, ref, sem).wait()


def flip(index, bits):
    for bit in range(bits.bit_length()):
        if bits >> bit & 1:
            index = index + 2**bit - 2 ** (bit + 1) * lax.rem(lax.div(index, 2**bit), 2)
    return index


def to_bf16(mask):
    return mask.astype(jnp.float32).astype(jnp.bfloat16)


def kernel(
    n_pages, n_blocks, qtok,
    q_hbm, cent_hbm, basis_hbm, ids_hbm, coef_hbm, count_hbm, cand_hbm, live_hbm, out_ref,
    cent, basis, ids, spots, coef, count, cand, live,
    qbuf, raw, emb, first, bound, outgo, income, scoreT, piece, landed,
    in_sem, q_send, q_recv, x_send, x_recv, aux_send, aux_recv, d_send, d_recv, e_send, e_recv,
):
    k = lax.axis_index("pages")
    r = lax.axis_index("blocks")
    core = lax.rem(k, 2)
    z = lax.div(k, 2)
    nz = n_pages // 2
    hz = nz // 2
    pages, patches = ids.shape
    cents, rank, width = basis.shape
    rows_q = q_hbm.shape[0]
    per_dev = rows_q // qtok
    per = DEPTH // rank
    slots, n_query = cand_hbm.shape
    half_rows = n_blocks * hz * rows_q
    block_rows = hz * rows_q

    own_row = (r * hz + lax.rem(z, hz)) * rows_q
    own = qbuf.at[pl.ds(pl.multiple_of(own_row, rows_q), rows_q), :]
    loads = [
        pltpu.make_async_copy(src, dst, in_sem.at[i])
        for i, (src, dst) in enumerate(
            [
                (q_hbm, own), (ids_hbm, spots), (ids_hbm, ids), (count_hbm, count.at[0]),
                (coef_hbm, coef), (cent_hbm, cent), (basis_hbm, basis),
                (cand_hbm, cand.at[0]), (live_hbm, live.at[0]),
            ]
        )
    ]
    for copy in loads:
        copy.start()

    barrier = pltpu.get_barrier_semaphore()
    peers = [(t, s) for t in range(nz) for s in range(n_blocks) if t or s]
    peers.sort(key=lambda ts: (-(ts[0] >= hz), -(ts[0].bit_count() + ts[1].bit_count())))
    places = {ts: (flip(z, ts[0]) * 2 + core, flip(r, ts[1])) for ts in peers}
    partner = (k + 1 - 2 * core, r)
    for where in [*places.values(), partner]:
        pl.semaphore_signal(barrier, inc=1, device_id=where, device_id_type=MESH)
    loads[0].wait()
    pl.semaphore_wait(barrier, len(peers) + 1)
    q_copies = []
    for ts in peers:
        start = own_row + (half_rows if ts[0] >= hz else 0)
        land = qbuf.at[pl.ds(pl.multiple_of(start, rows_q), rows_q), :]
        copy = remote(own, land, q_send, q_recv.at[int(ts[0] >= hz)], places[ts])
        copy.start()
        q_copies.append(copy)
    aux_copies = [
        remote(src, dst.at[1], aux_send.at[i], aux_recv.at[i], partner)
        for i, (src, dst) in enumerate([(count_hbm, count), (cand_hbm, cand), (live_hbm, live)])
    ]
    for copy in aux_copies:
        copy.start()

    for copy in loads[1:7]:
        copy.wait()

    diag = lax.broadcasted_iota(jnp.int32, (pages, pages), 0) == lax.broadcasted_iota(
        jnp.int32, (pages, pages), 1
    )

    def set_bound(a):
        spread = jnp.broadcast_to(count[a].astype(jnp.float32), (pages, pages))
        column = jnp.sum(jnp.where(diag, spread, 0.0), axis=1, keepdims=True)
        bound[a] = jnp.broadcast_to(column, (pages, width)) - (r * patches).astype(jnp.float32)

    set_bound(0)
    rows16 = 2 * per
    mix = lax.broadcasted_iota(jnp.int32, (rows16, DEPTH), 1)
    turn = lax.rem(lax.div(mix, rank) + per - lax.rem(lax.broadcasted_iota(jnp.int32, (rows16, DEPTH), 0), per), per)
    turn = turn.astype(jnp.float32).astype(jnp.bfloat16)
    page_low = lax.rem(lax.broadcasted_iota(jnp.int32, (pages, width), 0), per)
    id_lane = lax.broadcasted_iota(jnp.int32, (pages, patches), 1)
    id_low = lax.rem(lax.broadcasted_iota(jnp.int32, (pages, patches), 0), per)
    lane_id = lax.broadcasted_iota(jnp.int32, (pages, width), 1).astype(jnp.float32).astype(jnp.bfloat16)
    one = jnp.ones((pages, width), jnp.bfloat16)
    zero = jnp.zeros((pages, width), jnp.bfloat16)
    chunk_rows = per * pages
    turns = patches // per

    def emb_chunk(slot, c):
        return emb.at[slot, pl.ds(pl.multiple_of(c * chunk_rows, chunk_rows), chunk_rows), :]

    def swap(c):
        return remote(emb_chunk(0, c), emb_chunk(1, c), x_send, x_recv, partner)

    def decode(c, carry):
        id_f = ids[...].astype(jnp.float32)
        hots = []
        for s in range(per):
            target = c * per + lax.rem(id_low + s, per)
            mine = jnp.sum(jnp.where(id_lane == target, id_f, 0.0), axis=1, keepdims=True)
            mine = jnp.broadcast_to(mine, (pages, width)).astype(jnp.bfloat16)
            hots.append(
                jnp.concatenate(
                    [
                        jnp.where(mine == lane_id + jnp.bfloat16(t * width), one, zero)
                        for t in range(cents // width)
                    ],
                    axis=1,
                )
            )
        center = jnp.dot(jnp.concatenate(hots, axis=0), cent[...], preferred_element_type=jnp.float32)
        raw[...] = center.reshape(per, pages, width)
        for h in range(pages // rows16):
            top = h * rows16
            weights = coef[top : top + rows16, pl.ds(pl.multiple_of(c * DEPTH, DEPTH), DEPTH)]
            for s in range(per):
                lhs = jnp.where(turn == jnp.bfloat16(s), weights, jnp.zeros_like(weights))
                sides = []
                for g in range(2):
                    chosen = [
                        basis[spots[top + g * per + (b - s) % per, c * per + b]] for b in range(per)
                    ]
                    sides.append(jnp.concatenate(chosen, axis=0))
                rhs = jnp.concatenate(sides, axis=1)
                res = jnp.dot(lhs, rhs, preferred_element_type=jnp.float32)
                both = jnp.concatenate([res[:per, :width], res[per:, width:]], axis=0)
                raw[s, top : top + rows16, :] = raw[s, top : top + rows16, :] + both

        @pl.when(c == 0)
        def _():
            start = raw[0]
            for s in range(1, per):
                start = jnp.where(page_low == per - s, raw[s], start)
            first[...] = start

        for s in range(per):
            position = (c * per + lax.rem(page_low + s, per)).astype(jnp.float32)
            total = jnp.where(position < bound[0], raw[s], first[...])
            emb[0, pl.ds(pl.multiple_of(c * chunk_rows + s * pages, pages), pages), :] = total.astype(jnp.bfloat16)

        @pl.when(c > 0)
        def _():
            swap(c - 1).start()

        return carry

    lax.fori_loop(0, turns, decode, 0)
    pad = -(-block_rows // 128) * 128
    aux_copies[0].wait_recv()
    set_bound(1)
    swap(turns - 1).start()

    spot = lax.broadcasted_iota(jnp.int32, (1, pad), 1)
    seen = lax.broadcasted_iota(jnp.int32, (n_query, pad), 0)

    def gather(h):
        away = flip(z, h * hz)
        z_abs = lax.div(away, hz) * hz + lax.div(spot, rows_q)
        index = ((z_abs * 2 + core) * n_blocks + r) * per_dev + lax.div(lax.rem(spot, rows_q), qtok)
        index = jnp.where(spot < block_rows, index, -1)
        return to_bf16(index == seen)

    blocks_at_once = min(n_blocks, max(1, GROUP // block_rows))
    cols = blocks_at_once * block_rows
    rows = STEP * pages

    def score(h, a):
        for b in range(0, n_blocks, blocks_at_once):
            begin = h * half_rows + b * block_rows
            query = qbuf[begin : begin + cols, :]
            best = jnp.full((pages, cols), LOWEST, jnp.float32)
            for m in range(patches // STEP):
                sim = lax.dot_general(
                    emb[a, m * rows : (m + 1) * rows, :], query, (((1,), (1,)), ((), ())),
                    preferred_element_type=jnp.float32,
                )
                best = jnp.maximum(best, jnp.max(sim.reshape(STEP, pages, cols), axis=0))
            best = jnp.where(bound[a][:, :1] > 0.0, best, LOWEST)
            for i in range(blocks_at_once):
                part = best[:, i * block_rows : (i + 1) * block_rows]
                if pad > block_rows:
                    part = jnp.concatenate([part, jnp.zeros((pages, pad - block_rows), jnp.float32)], axis=1)
                outgo[h * n_blocks + b + i, a * pages : (a + 1) * pages, :] = part.astype(jnp.bfloat16)

    d_copies = []

    def reduce_start(h):
        for s in sorted(range(1, n_blocks), key=lambda s: -s.bit_count()):
            copy = remote(
                outgo.at[h * n_blocks + flip(r, s)], income.at[h * n_blocks + s],
                d_send, d_recv.at[h], (k, flip(r, s)),
            )
            copy.start()
            d_copies.append(copy)

    def reduce_end(h):
        arrived(income.at[h * n_blocks + 1 : (h + 1) * n_blocks], d_recv.at[h])
        highest = outgo[h * n_blocks + r].astype(jnp.float32)
        for s in range(1, n_blocks):
            highest = jnp.maximum(highest, income[h * n_blocks + s].astype(jnp.float32))
        return lax.dot_general(
            highest.astype(jnp.bfloat16), gather(h), (((1,), (1,)), ((), ())),
            preferred_element_type=jnp.float32,
        )

    arrived(qbuf.at[0 : half_rows - rows_q], q_recv.at[0])
    score(0, 0)
    arrived(emb.at[1], x_recv)
    score(0, 1)
    reduce_start(0)
    for copy in [*loads[7:]]:
        copy.wait()
    for copy in aux_copies[1:]:
        copy.wait_recv()
    arrived(qbuf.at[half_rows : 2 * half_rows], q_recv.at[1])
    score(1, 0)
    score(1, 1)
    reduce_start(1)
    sums = reduce_end(0)
    sums = sums + reduce_end(1)

    slot = lax.broadcasted_iota(jnp.int32, (slots, n_query), 0)
    picks = []
    for a in range(2):
        chosen = cand[a]
        picked = jnp.zeros((slots, n_query), jnp.float32)
        for n in range(pages):
            picked = jnp.where(chosen == n, sums[a * pages + n : a * pages + n + 1, :], picked)
        picks.append(jnp.where(slot < live[a], picked, 0.0))
    even = core == 0
    wide_q = scoreT.shape[0]
    stacked = []
    for low, high in (picks, picks[::-1]):
        tall = jnp.where(even, low, high)
        stacked += [tall, jnp.zeros((width // 2 - slots, n_query), jnp.float32)]
    full = jnp.concatenate(stacked, axis=0)
    if wide_q > n_query:
        full = jnp.concatenate([full, jnp.zeros((width, wide_q - n_query), jnp.float32)], axis=1)
    scoreT[...] = full.T

    e_copies = []
    for t in range(nz - 1, -1, -1):
        to = flip(z, t)
        values = scoreT[pl.ds(((to * 2 + core) * n_blocks + r) * per_dev, per_dev), :]
        if t == 0:
            landed[z] = values
        else:
            piece[t] = values
            copy = remote(piece.at[t], landed.at[z], e_send, e_recv, (to * 2 + core, r))
            copy.start()
            e_copies.append(copy)
    total_q = len(peers) * rows_q
    arrived(qbuf.at[0:total_q], q_send)
    arrived(emb.at[0], x_send)
    arrived(income.at[0 : len(d_copies)], d_send)
    for copy in aux_copies:
        copy.wait_send()
    arrived(landed.at[1:nz], e_recv)
    for zs in range(nz):
        values = landed[zs]
        for p in range(2):
            for i in range(per_dev):
                out_ref[i, 2 * zs + p : 2 * zs + p + 1, :] = values[
                    i : i + 1, p * (width // 2) : p * (width // 2) + slots
                ]
    arrived(piece.at[1:nz], e_send)


def on_device(queries, centroids, basis, patch_ids, coeffs, page_counts, cand_ids, cand_counts):
    n_pages = lax.axis_size("pages")
    n_blocks = lax.axis_size("blocks")
    owned, qtok, width = queries.shape
    cents, rank, _ = basis.shape
    _, pages, patches = patch_ids.shape
    _, n_query, slots = cand_ids.shape
    rows_q = owned * qtok
    nz = n_pages // 2
    block_rows = nz // 2 * rows_q
    pad = -(-block_rows // 128) * 128
    args = (
        queries.reshape(rows_q, width),
        centroids,
        basis,
        patch_ids[0],
        coeffs[0],
        page_counts,
        jnp.swapaxes(cand_ids[0], 0, 1),
        cand_counts,
    )
    dma = pltpu.SemaphoreType.DMA
    bf16, f32, i32 = jnp.bfloat16, jnp.float32, jnp.int32
    vmem = pltpu.VMEM
    totals = pl.pallas_call(
        functools.partial(kernel, n_pages, n_blocks, qtok),
        out_shape=vmem((owned, n_pages, slots), f32),
        in_specs=[pl.BlockSpec(memory_space=pl.ANY)] * len(args),
        out_specs=pl.BlockSpec(memory_space=pltpu.VMEM),
        scratch_shapes=[
            vmem((cents, width), bf16),
            vmem((cents, rank, width), bf16),
            vmem((pages, patches), i32),
            pltpu.SMEM((pages, patches), i32),
            vmem((pages, patches * rank), bf16),
            vmem((2, 1, pages), i32),
            vmem((2, slots, n_query), i32),
            vmem((2, 1, n_query), i32),
            vmem((n_blocks * nz * rows_q, width), bf16),
            vmem((DEPTH // rank, pages, width), f32),
            vmem((2, patches * pages, width), bf16),
            vmem((pages, width), f32),
            vmem((2, pages, width), f32),
            vmem((2 * n_blocks, 2 * pages, pad), bf16),
            vmem((2 * n_blocks, 2 * pages, pad), bf16),
            vmem((-(-n_query // 128) * 128, width), f32),
            vmem((nz, owned, width), f32),
            vmem((nz, owned, width), f32),
            dma((9,)),
            dma, dma((2,)),
            dma, dma,
            dma((3,)), dma((3,)),
            dma, dma((2,)),
            dma, dma,
        ],
        compiler_params=pltpu.CompilerParams(collective_id=0, has_side_effects=True),
    )(*args)
    return totals / qtok


def solution(mesh):
    placed = (
        P(("pages", "blocks"), None, None),
        P(),
        P(),
        P("pages", None, "blocks"),
        P("pages", None, "blocks"),
        P("pages", None),
        P("pages", None, None),
        P("pages", None),
    )
    return jax.shard_map(
        on_device,
        mesh=mesh,
        in_specs=placed,
        out_specs=P(("pages", "blocks"), None, None),
        check_vma=False,
    )
```

time: 24 us -> 21.7 us (0.904)
  Pallas kernels: 23.1 us -> 20.8 us
    pallas_call x1, Pallas kernels: 23.1 us -> 20.8 us  [on_device(): pl.pallas_call(functools.partial(kernel, n_pages, n_blocks, qtok), out_sh...]
where the time goes in v2:
time: 21.7 us; the launch traced here: 21.4 us
  Pallas kernels  20.8 us (96%)
  other arithmetic  0.6 us (3%)
    pallas_call x1, Pallas kernels, on_device(): pl.pallas_call(functools.partial(kernel, n_pages, n_blocks, qtok), out_sh...  20.8 us
    div x1, other arithmetic, on_device(): return totals / qtok  0.6 us

profile of v2, /device:TPU:0, one launch (start us, length us, event | category | flops | bytes accessed | tf_op | source)
XLA Modules:
  0.0 21.4 jit_solution(10410527146412894517)
XLA Ops:
  0.0 20.8 %shard_map.82 = f32[2,8,16]{2,1,0:T(8,128)S(1)} custom-call(bf16[48,128]{1,0:T(8,128)(2,1)} %bitcast.8, bf16[256,128]{1,0:T(8,128)(2,1)} %cent_hbm.1, bf16[256,32,128]{2,1,0:T(8,128)(2,1)} %basis_hbm.1, s32[32,64]{1,0:T(8,128)} %bitcast.7, bf16[32,2048]{1,0:T(8,128)(2,1)} %bitcast.6, s32[1,32]{1,0:T(1,128)} %count_hbm.1, s32[16,64]{1,0:T(8,128)} %bitcast.9, ...), custom_call_target="tpu_custom_call" | custom-call | tf_op jit(solution)/shard_map/pallas_call | solution.py:328
  20.8 0.6 %broadcast_multiply_fusion = f32[2,8,16]{2,1,0:T(8,128)} fusion(f32[2,8,16]{2,1,0:T(8,128)S(1)} %shard_map.82), kind=kLoop, calls=%fused_computation | loop fusion | flops 256 | bytes 2048 | tf_op jit(solution)/shard_map/div | solution.py:361
